TPU v7x, 256 devices: a whole 4x4x8 slice. The times are simulated.
256 devices in a mesh: space: 32 (over x, y, core), tm: 8 (over z).
Axes of the slice: x: 4, y: 4, z: 8, core: 2. Of those that a mesh axis runs over, the one named last changes fastest.
Arguments:
- velocity: bfloat16 [256, 2, 512, 1024], P('tm', None, 'space'), may hold values from -8.4 to 8.4
Outputs:
- vorticity: bfloat16 [256, 512, 1024], P('tm', 'space')
- modes: float32 [32, 512, 1024], P('tm', 'space')
All inputs are finite; a program needn't handle non-finite values.
Results may differ from a plain program's by a relative error of at most 0.003.
Values may be sent and summed in bfloat16 or wider, within the bound.
A program may use at most 64 MiB of HBM per device.

v0:
```python
import jax
import jax.numpy as jnp
from jax import lax
from jax.sharding import PartitionSpec as P

RANK = 32
HIGH = lax.Precision.HIGHEST


def halo_rows(block, width):
    count = lax.axis_size("space")
    forward = [(i, (i + 1) % count) for i in range(count)]
    backward = [(target, source) for source, target in forward]
    rows = block.shape[1]
    low = lax.ppermute(block[:, rows - width :], "space", forward)
    high = lax.ppermute(block[:, :width], "space", backward)
    return jnp.concatenate([low, block, high], axis=1)


def spanwise(field):
    ahead = jnp.roll(field, -1, 2)
    behind = jnp.roll(field, 1, 2)
    ahead_two = jnp.roll(field, -2, 2)
    behind_two = jnp.roll(field, 2, 2)
    return (8.0 * (ahead - behind) - (ahead_two - behind_two)) / 12.0


def merge_small(gram):
    coeffs = gram[:, :, :RANK] + gram[:, :, RANK:]
    diagonal = jnp.diagonal(gram, axis1=1, axis2=2)
    scales = jnp.sqrt(diagonal[:, :RANK] + diagonal[:, RANK:])
    half = jnp.einsum("nab,nbc->nac", gram, coeffs, precision=HIGH)
    inner = jnp.einsum("nab,nac->nbc", coeffs, half, precision=HIGH)
    lower = jnp.linalg.cholesky(inner)
    eye = jnp.broadcast_to(jnp.eye(RANK, dtype=jnp.float32), inner.shape)
    lower_inv = lax.linalg.triangular_solve(lower, eye, left_side=True, lower=True)
    factor = jnp.swapaxes(lower_inv, 1, 2) * scales[:, None, :]
    return jnp.einsum("nab,nbc->nac", coeffs, factor, precision=HIGH)


def tree_basis(gram, leaves):
    width = leaves * RANK
    basis = None
    span = 1
    while span < leaves:
        nodes = leaves // (2 * span)
        size = 2 * span * RANK
        sub = jnp.stack(
            [gram[k * size : (k + 1) * size, k * size : (k + 1) * size] for k in range(nodes)]
        )
        if basis is None:
            h = sub
        else:
            b = basis.reshape(nodes, 2, span * RANK, RANK)
            zero = jnp.zeros_like(b[:, 0])
            bd = jnp.concatenate(
                [
                    jnp.concatenate([b[:, 0], zero], axis=2),
                    jnp.concatenate([zero, b[:, 1]], axis=2),
                ],
                axis=1,
            )
            gb = jnp.einsum("nab,nbc->nac", sub, bd, precision=HIGH)
            h = jnp.einsum("nab,nac->nbc", bd, gb, precision=HIGH)
        c = merge_small(h)
        if basis is None:
            basis = c
        else:
            basis = jnp.einsum("nab,nbc->nac", bd, c, precision=HIGH)
        span *= 2
    return basis.reshape(width, RANK)


def local(velocity):
    rows = velocity.shape[2]
    span_v = halo_rows(velocity[:, 1], 2).astype(jnp.float32)
    stream_u = velocity[:, 0].astype(jnp.float32)
    dv_dx = (
        8.0 * (span_v[:, 3 : rows + 3] - span_v[:, 1 : rows + 1])
        - (span_v[:, 4:] - span_v[:, :rows])
    ) / 12.0
    vorticity = (dv_dx - spanwise(stream_u)).astype(jnp.bfloat16)
    blocks = lax.axis_size("tm")
    cells = lax.all_to_all(vorticity, "tm", 2, 0, tiled=True)
    flat = cells.reshape(cells.shape[0], -1)
    gram = jnp.einsum("ax,bx->ab", flat, flat, preferred_element_type=jnp.float32)
    gram = lax.psum(gram, ("space", "tm"))
    basis = tree_basis(gram, blocks)
    part = jnp.einsum("ab,ax->bx", basis, flat.astype(jnp.float32), precision=HIGH).reshape(
        RANK, rows, -1
    )
    modes = lax.all_to_all(part, "tm", 0, 2, tiled=True)
    return (vorticity, modes)


def solution(mesh):
    in_specs = (P("tm", None, "space", None),)
    out_specs = (P("tm", "space", None), P("tm", "space", None))
    return jax.shard_map(local, mesh=mesh, in_specs=in_specs, out_specs=out_specs, check_vma=False)
```

profile of v0, /device:TPU:2, one launch (start us, length us, event | category | flops | bytes accessed | tf_op | source)
XLA Modules:
  0.0 411.2 jit_solution(9131504356403751906)
XLA Ops:
  7.2 1.9 bitcast_convert_fusion
  9.0 0.6 copy.179
  9.6 0.1 collective-permute-start
  9.7 3.8 collective-permute-start.1
  13.6 0.7 fusion.72
  14.3 0.7 fusion.74
  15.1 0.1 fusion.73
  15.2 0.1 fusion.71
  15.4 0.8 collective-permute-done
  16.2 0.2 pad_maximum_fusion
  16.4 0.8 copy_convert_fusion
  17.2 2.2 fusion.3
  19.4 5.1 %copy.130 = bf16[32,16,1024]{0,1,2:T(8,128)(2,1)} copy(bf16[32,16,1024]{2,1,0:T(8,128)(2,1)S(1)} %fusion.3) | data formatting | bytes 2097152 | tf_op jit(solution)/shard_map/convert_element_type | solution.py:82
  24.5 7.8 %reshape.157 = bf16[8,2,32768]{2,1,0:T(2,128)(2,1)} reshape(bf16[1024,16,32]{2,1,0:T(8,128)(2,1)} %bitcast.133) | data formatting | bytes 2097152
  32.4 8.5 %all-to-all-start = ((bf16[8,2,32768]{2,1,0:T(2,128)(2,1)}), bf16[8,2,32768]{2,1,0:T(2,128)(2,1)S(1)}, u32[]{:S(2)}, u32[]{:S(2)}) async-start(bf16[8,2,32768]{2,1,0:T(2,128)(2,1)} %reshape.157), calls=%async_computation | async-start | bytes 2097152 | tf_op jit(solution)/shard_map/all_to_all | solution.py:84
  40.8 0.2 all-reduce.6.cloned.1.call-start
  41.1 28.5 %all-to-all-done = bf16[8,2,32768]{2,1,0:T(2,128)(2,1)S(1)} async-done(((bf16[8,2,32768]{2,1,0:T(2,128)(2,1)}), bf16[8,2,32768]{2,1,0:T(2,128)(2,1)S(1)}, u32[]{:S(2)}, u32[]{:S(2)}) %all-to-all-start) | async-done | bytes 1048608 | tf_op jit(solution)/shard_map/all_to_all | solution.py:84
  69.6 4.5 %reshape.158 = bf16[1024,16,32]{2,1,0:T(8,128)(2,1)} reshape(bf16[8,2,32768]{2,1,0:T(2,128)(2,1)S(1)} %all-to-all-done) | data formatting | bytes 2097152
  74.1 5.4 %copy.131 = bf16[32,16,8,128]{3,1,0,2:T(8,128)(2,1)S(1)} copy(bf16[32,16,8,128]{0,1,3,2:T(8,128)(2,1)} %bitcast.132) | data formatting | bytes 2097152 | tf_op jit(solution)/shard_map/all_to_all | solution.py:84
  79.5 1.2 fusion.10
  80.7 0.7 copy.133
  81.4 0.3 copy.178
  81.7 0.5 copy.152
  82.2 244.6 %all-reduce.6.cloned.1.call-done = f32[256,256]{0,1:T(8,128)} async-done(((f32[256,256]{0,1:T(8,128)}), f32[256,256]{0,1:T(8,128)}) %all-reduce.6.cloned.1.call-update) | async-done | bytes 262160 | tf_op jit(solution)/shard_map/psum | solution.py:87
  326.8 0.9 slice_bitcast_fusion.7
  327.8 1.9 copy.137
  329.7 0.9 fusion.70
  330.6 1.5 gather_fusion
  332.0 0.8 copy.138
  332.9 1.1 fusion.69
  334.1 11.7 %custom-call.21 = f32[4,32,32]{2,1,0:T(8,128)S(1)} custom-call(f32[4,32,32]{2,1,0:T(8,128)S(1)} %fusion.19), custom_call_target="Cholesky" | custom-call | tf_op jit(solution)/shard_map/jit(cholesky)/cholesky | solution.py:34
  345.9 0.1 compare_reduce_fusion.2
  346.1 9.8 %custom-call.22 = f32[4,1,32,32]{2,3,1,0:T(8,128)S(1)} custom-call(f32[4,1,32,32]{3,2,1,0:T(8,128)S(1)} %select_bitcast_fusion), custom_call_target="InvertDiagBlocksLowerTriangular" | custom-call | tf_op jit(solution)/shard_map/triangular_solve | solution.py:36
  355.9 0.9 convolution_multiply_fusion
  356.9 0.3 fusion.68
  357.2 0.3 fusion.13
  357.5 0.3 fusion.39
  357.8 1.9 copy.147
  359.7 0.8 fusion.67
  360.5 1.5 gather_fusion.1
  362.0 0.8 copy.148
  362.9 0.9 fusion.66
  363.9 5.9 %custom-call.23 = f32[2,32,32]{2,1,0:T(8,128)S(1)} custom-call(f32[2,32,32]{2,1,0:T(8,128)S(1)} %fusion.32), custom_call_target="Cholesky" | custom-call | tf_op jit(solution)/shard_map/jit(cholesky)/cholesky | solution.py:34
  369.8 0.1 compare_reduce_fusion.1
  370.0 4.9 %custom-call.24 = f32[2,1,32,32]{2,3,1,0:T(8,128)S(1)} custom-call(f32[2,1,32,32]{3,2,1,0:T(8,128)S(1)} %select_bitcast_fusion.1), custom_call_target="InvertDiagBlocksLowerTriangular" | custom-call | tf_op jit(solution)/shard_map/triangular_solve | solution.py:36
  375.0 0.9 convolution_multiply_fusion.1
  375.9 0.2 fusion.65
  376.1 0.2 convolution_bitcast_fusion.1
  376.4 0.3 fusion.23
  376.7 0.2 fusion.21
  376.9 0.8 gather_fusion.2
  377.7 0.1 fusion.63
  377.8 0.1 fusion.61
  378.1 2.9 custom-call.25
  381.0 0.6 compare_reduce_fusion
  381.7 0.7 fusion.34
  382.3 2.4 custom-call.26
  384.8 0.2 fusion.9
  385.0 0.2 fusion.59
  385.2 0.2 convolution_bitcast_fusion
  385.4 1.0 fusion.76
  386.4 0.2 copy.153
  386.6 17.1 %all_to_all.33 = f32[32,16,128]{2,1,0:T(8,128)S(1)} all-to-all(f32[32,16,128]{2,1,0:T(8,128)S(1)} %copy.153), channel_id=1, replica_groups=mesh['space'=32,'tm'=8] {'tm'}, dimensions={0} | all-to-all | bytes 524288 | tf_op jit(solution)/shard_map/all_to_all | solution.py:92
  403.7 0.7 copy.180
  (29 shorter events, 0.9 us)
Async XLA Ops:
  9.6 6.6 %collective-permute-start = (bf16[32,2,1024]{2,0,1:T(8,128)(2,1)S(1)}, bf16[32,2,1024]{2,0,1:T(8,128)(2,1)S(1)}, u32[]{:S(2)}, u32[]{:S(2)}) collective-permute-start(bf16[32,2,1024]{2,0,1:T(8,128)(2,1)S(1)} %get-tuple-element.18), channel_id=1, source_target_pairs={{0,8},{8,16},{16,24},{24,32},{32,40},{40,48},{48,56},{56,64},{64,7... | collective-permute-start | bytes 393224 | tf_op jit(solution)/shard_map/ppermute | solution.py:15
  9.7 6.5 %collective-permute-start.1 = (bf16[32,2,1024]{2,0,1:T(8,128)(2,1)S(1)}, bf16[32,2,1024]{2,0,1:T(8,128)(2,1)S(1)}, u32[]{:S(2)}, u32[]{:S(2)}) collective-permute-start(bf16[32,2,1024]{2,0,1:T(8,128)(2,1)S(1)} %get-tuple-element.19), channel_id=1, source_target_pairs={{8,0},{16,8},{24,16},{32,24},{40,32},{48,40},{56,48},{64,56},{72,6... | collective-permute-start | bytes 393224 | tf_op jit(solution)/shard_map/ppermute | solution.py:16
  19.4 5.1 %copy-start = (bf16[32,16,1024]{2,1,0:T(8,128)(2,1)}, bf16[32,16,1024]{2,1,0:T(8,128)(2,1)S(1)}, u32[]{:S(2)}) copy-start(bf16[32,16,1024]{2,1,0:T(8,128)(2,1)S(1)} %fusion.3) | copy-start | bytes 3145732
  32.4 37.2 %all-to-all-start = ((bf16[8,2,32768]{2,1,0:T(2,128)(2,1)}), bf16[8,2,32768]{2,1,0:T(2,128)(2,1)S(1)}, u32[]{:S(2)}, u32[]{:S(2)}) async-start(bf16[8,2,32768]{2,1,0:T(2,128)(2,1)} %reshape.157), calls=%async_computation | async-start | bytes 2097152 | tf_op jit(solution)/shard_map/all_to_all | solution.py:84
  40.8 286.0 %all-reduce.6.cloned.1.call-start = ((), (), s32[]{:S(2)}) async-start(), calls=%async_computation.2 | async-start | bytes 524288 | tf_op jit(solution)/shard_map/psum | solution.py:87
  327.7 29.5 %copy-start.1 = (f32[256,256]{0,1:T(8,128)S(1)}, f32[256,256]{0,1:T(8,128)}, u32[]{:S(2)}) copy-start(f32[256,256]{0,1:T(8,128)} %all-reduce.6.cloned.1.call-done) | copy-start | bytes 786436
Sparse Core Ops, SparseCore 0:
  80.8 245.9 all-reduce.5
where the time goes:
time: 412 us; the launch traced here: 411 us
  waiting for transfers between devices  274 us (67%)
  other arithmetic  44.8 us (11%)
  local copies, waits for them, and re-layouts  37.9 us (9%)
  blocking collectives  17.1 us (4%)
  between operations  14.4 us (3%)
  starting transfers between devices  12.6 us (3%)
  matrix products  10.4 us (3%)
    psum x1, waiting for transfers between devices, local(): gram = lax.psum(gram, ('space', 'tm'))  245 us
    all_to_all x1, waiting for transfers between devices, local(): cells = lax.all_to_all(vorticity, 'tm', 2, 0, tiled=True)  28.5 us
    another operation x9, other arithmetic, merge_small(): lower = jnp.linalg.cholesky(inner)  21.5 us
    another operation x7, other arithmetic, merge_small(): lax.linalg.triangular_solve(lower, eye, left_side=True, lower=True)  18 us
    all_to_all x1, blocking collectives, local(): modes = lax.all_to_all(part, 'tm', 0, 2, tiled=True)  17.1 us
    unnamed x8, local copies, waits for them, and re-layouts  13.2 us
    all_to_all x1, starting transfers between devices, local(): cells = lax.all_to_all(vorticity, 'tm', 2, 0, tiled=True)  8.47 us
  transfers between devices with their start and end apart: 4, of which 3 were waited for; matrix products, arithmetic and copies ran while one was open for 1% of the time, Pallas kernels for 0%

commit v1 on v0

--- a/solution.py
+++ b/solution.py
@@ -84,7 +84,7 @@
     cells = lax.all_to_all(vorticity, "tm", 2, 0, tiled=True)
     flat = cells.reshape(cells.shape[0], -1)
     gram = jnp.einsum("ax,bx->ab", flat, flat, preferred_element_type=jnp.float32)
-    gram = lax.psum(gram, ("space", "tm"))
+    gram = lax.psum(lax.psum(gram, "space"), "tm")
     basis = tree_basis(gram, blocks)
     part = jnp.einsum("ab,ax->bx", basis, flat.astype(jnp.float32), precision=HIGH).reshape(
         RANK, rows, -1

time: 412 us -> 344 us (0.83)
  waiting for transfers between devices: 274 us -> 181 us
  blocking collectives: 17.1 us -> 51.5 us
  starting transfers between devices: 12.6 us -> 4.18 us
    psum x1 -> x2, waiting for transfers between devices: 245 us -> 180 us  [local(): gram = lax.psum(lax.psum(gram, 'space'), 'tm')]
    all_to_all x0 -> x1, blocking collectives: none -> 37 us  [local(): cells = lax.all_to_all(vorticity, 'tm', 2, 0, tiled=True)]
    all_to_all x1 -> x0, waiting for transfers between devices: 28.5 us -> none  [local(): cells = lax.all_to_all(vorticity, 'tm', 2, 0, tiled=True)]
    all_to_all x1 -> x0, starting transfers between devices: 8.47 us -> none  [local(): cells = lax.all_to_all(vorticity, 'tm', 2, 0, tiled=True)]
where the time goes in v1:
time: 344 us; the launch traced here: 343 us
  waiting for transfers between devices  181 us (53%)
  blocking collectives  51.5 us (15%)
  other arithmetic  44.8 us (13%)
  local copies, waits for them, and re-layouts  37.1 us (11%)
  between operations  14.4 us (4%)
  matrix products  10.4 us (3%)
  starting transfers between devices  4.18 us (1%)
    psum x2, waiting for transfers between devices, local(): gram = lax.psum(lax.psum(gram, 'space'), 'tm')  180 us
    all_to_all x1, blocking collectives, local(): cells = lax.all_to_all(vorticity, 'tm', 2, 0, tiled=True)  37 us
    another operation x9, other arithmetic, merge_small(): lower = jnp.linalg.cholesky(inner)  21.5 us
    another operation x7, other arithmetic, merge_small(): lax.linalg.triangular_solve(lower, eye, left_side=True, lower=True)  18 us
    all_to_all x1, blocking collectives, local(): modes = lax.all_to_all(part, 'tm', 0, 2, tiled=True)  14.4 us
    unnamed x8, local copies, waits for them, and re-layouts  12.4 us
  transfers between devices with their start and end apart: 4, of which 3 were waited for; matrix products, arithmetic and copies ran while one was open for 1% of the time, Pallas kernels for 0%

profile of v1, /device:TPU:2, one launch (start us, length us, event | category | flops | bytes accessed | tf_op | source)
XLA Modules:
  0.0 343.2 jit_solution(257742224501949670)
XLA Ops:
  7.2 1.9 bitcast_convert_fusion
  9.1 0.6 copy.179
  9.7 0.1 collective-permute-start
  9.8 3.8 %collective-permute-start.1 = (bf16[32,2,1024]{2,0,1:T(8,128)(2,1)S(1)}, bf16[32,2,1024]{2,0,1:T(8,128)(2,1)S(1)}, u32[]{:S(2)}, u32[]{:S(2)}) collective-permute-start(bf16[32,2,1024]{2,0,1:T(8,128)(2,1)S(1)} %get-tuple-element.19), channel_id=1, source_target_pairs={{8,0},{16,8},{24,16},{32,24},{40,32},{48,40},{56,48},{64,56},{72,6... | collective-permute-start | bytes 393224 | tf_op jit(solution)/shard_map/ppermute | solution.py:16
  13.6 0.7 fusion.72
  14.4 0.7 fusion.74
  15.1 0.1 fusion.73
  15.3 0.1 fusion.71
  15.4 0.8 collective-permute-done
  16.3 0.2 pad_maximum_fusion
  16.4 0.8 copy_convert_fusion
  17.2 2.2 fusion.3
  19.5 5.1 %copy.130 = bf16[32,16,1024]{0,1,2:T(8,128)(2,1)} copy(bf16[32,16,1024]{2,1,0:T(8,128)(2,1)S(1)} %fusion.3) | data formatting | bytes 2097152 | tf_op jit(solution)/shard_map/convert_element_type | solution.py:82
  24.6 7.0 %reshape.157 = bf16[8,2,32768]{2,1,0:T(2,128)(2,1)S(1)} reshape(bf16[1024,16,32]{2,1,0:T(8,128)(2,1)} %bitcast.133) | data formatting | bytes 2097152
  31.6 37.0 %all_to_all.33 = bf16[8,2,32768]{2,1,0:T(2,128)(2,1)S(1)} all-to-all(bf16[8,2,32768]{2,1,0:T(2,128)(2,1)S(1)} %reshape.157), channel_id=1, replica_groups=mesh['space'=32,'tm'=8] {'tm'}, dimensions={0} | all-to-all | bytes 2097152 | tf_op jit(solution)/shard_map/all_to_all | solution.py:84
  68.6 4.5 %reshape.158 = bf16[1024,16,32]{2,1,0:T(8,128)(2,1)} reshape(bf16[8,2,32768]{2,1,0:T(2,128)(2,1)S(1)} %all_to_all.33) | data formatting | bytes 2097152
  73.1 5.4 %copy.131 = bf16[32,16,8,128]{3,1,0,2:T(8,128)(2,1)S(1)} copy(bf16[32,16,8,128]{0,1,3,2:T(8,128)(2,1)} %bitcast.132) | data formatting | bytes 2097152 | tf_op jit(solution)/shard_map/all_to_all | solution.py:84
  78.5 1.2 fusion.10
  79.7 0.2 all-reduce.9.cloned.1.call-start
  79.9 106.4 %all-reduce.7.cloned.1.call-done = f32[256,256]{0,1:T(8,128)} async-done(((f32[256,256]{0,1:T(8,128)}), f32[256,256]{0,1:T(8,128)}) %all-reduce.7.cloned.1.call-update) | async-done | bytes 262160 | tf_op jit(solution)/shard_map/psum | solution.py:87
  186.4 0.7 copy.133
  187.1 0.3 copy.178
  187.3 0.5 copy.152
  187.9 73.6 %all-reduce.9.cloned.1.call-done = f32[256,256]{0,1:T(8,128)} async-done(((f32[256,256]{0,1:T(8,128)}), f32[256,256]{0,1:T(8,128)}) %all-reduce.9.cloned.1.call-update) | async-done | bytes 262160 | tf_op jit(solution)/shard_map/psum | solution.py:87
  261.5 0.9 slice_bitcast_fusion.7
  262.4 1.9 copy.137
  264.3 0.9 fusion.70
  265.2 1.5 gather_fusion
  266.6 0.8 copy.138
  267.5 1.1 fusion.69
  268.7 11.7 %custom-call.21 = f32[4,32,32]{2,1,0:T(8,128)S(1)} custom-call(f32[4,32,32]{2,1,0:T(8,128)S(1)} %fusion.19), custom_call_target="Cholesky" | custom-call | tf_op jit(solution)/shard_map/jit(cholesky)/cholesky | solution.py:34
  280.5 0.1 compare_reduce_fusion.2
  280.7 9.8 %custom-call.22 = f32[4,1,32,32]{2,3,1,0:T(8,128)S(1)} custom-call(f32[4,1,32,32]{3,2,1,0:T(8,128)S(1)} %select_bitcast_fusion), custom_call_target="InvertDiagBlocksLowerTriangular" | custom-call | tf_op jit(solution)/shard_map/triangular_solve | solution.py:36
  290.5 0.9 convolution_multiply_fusion
  291.5 0.3 fusion.68
  291.8 0.3 fusion.13
  292.1 0.3 fusion.39
  292.4 1.9 copy.147
  294.3 0.8 fusion.67
  295.1 1.5 gather_fusion.1
  296.6 0.8 copy.148
  297.5 0.9 fusion.66
  298.6 5.9 %custom-call.23 = f32[2,32,32]{2,1,0:T(8,128)S(1)} custom-call(f32[2,32,32]{2,1,0:T(8,128)S(1)} %fusion.32), custom_call_target="Cholesky" | custom-call | tf_op jit(solution)/shard_map/jit(cholesky)/cholesky | solution.py:34
  304.5 0.1 compare_reduce_fusion.1
  304.7 4.9 %custom-call.24 = f32[2,1,32,32]{2,3,1,0:T(8,128)S(1)} custom-call(f32[2,1,32,32]{3,2,1,0:T(8,128)S(1)} %select_bitcast_fusion.1), custom_call_target="InvertDiagBlocksLowerTriangular" | custom-call | tf_op jit(solution)/shard_map/triangular_solve | solution.py:36
  309.6 0.9 convolution_multiply_fusion.1
  310.5 0.2 fusion.65
  310.7 0.2 convolution_bitcast_fusion.1
  311.0 0.3 fusion.23
  311.3 0.2 fusion.21
  311.5 0.8 gather_fusion.2
  312.3 0.1 fusion.63
  312.4 0.1 fusion.61
  312.7 2.9 custom-call.25
  315.6 0.6 compare_reduce_fusion
  316.3 0.7 fusion.34
  316.9 2.4 custom-call.26
  319.4 0.2 fusion.9
  319.7 0.2 fusion.59
  319.8 0.2 convolution_bitcast_fusion
  320.0 1.0 fusion.76
  321.0 0.2 copy.153
  321.2 14.4 %all_to_all.34 = f32[32,16,128]{2,1,0:T(8,128)S(1)} all-to-all(f32[32,16,128]{2,1,0:T(8,128)S(1)} %copy.153), channel_id=1, replica_groups=mesh['space'=32,'tm'=8] {'tm'}, dimensions={0} | all-to-all | bytes 524288 | tf_op jit(solution)/shard_map/all_to_all | solution.py:92
  335.6 0.7 copy.180
  (31 shorter events, 0.9 us)
Async XLA Ops:
  7.2 179.2 %all-reduce.7.cloned.1.call-start = ((), (), s32[]{:S(2)}) async-start(), calls=%async_computation.2 | async-start | bytes 524288 | tf_op jit(solution)/shard_map/psum | solution.py:87
  9.7 6.6 %collective-permute-start = (bf16[32,2,1024]{2,0,1:T(8,128)(2,1)S(1)}, bf16[32,2,1024]{2,0,1:T(8,128)(2,1)S(1)}, u32[]{:S(2)}, u32[]{:S(2)}) collective-permute-start(bf16[32,2,1024]{2,0,1:T(8,128)(2,1)S(1)} %get-tuple-element.18), channel_id=1, source_target_pairs={{0,8},{8,16},{16,24},{24,32},{32,40},{40,48},{48,56},{56,64},{64,7... | collective-permute-start | bytes 393224 | tf_op jit(solution)/shard_map/ppermute | solution.py:15
  9.8 6.5 %collective-permute-start.1 = (bf16[32,2,1024]{2,0,1:T(8,128)(2,1)S(1)}, bf16[32,2,1024]{2,0,1:T(8,128)(2,1)S(1)}, u32[]{:S(2)}, u32[]{:S(2)}) collective-permute-start(bf16[32,2,1024]{2,0,1:T(8,128)(2,1)S(1)} %get-tuple-element.19), channel_id=1, source_target_pairs={{8,0},{16,8},{24,16},{32,24},{40,32},{48,40},{56,48},{64,56},{72,6... | collective-permute-start | bytes 393224 | tf_op jit(solution)/shard_map/ppermute | solution.py:16
  19.5 5.1 %copy-start = (bf16[32,16,1024]{2,1,0:T(8,128)(2,1)}, bf16[32,16,1024]{2,1,0:T(8,128)(2,1)S(1)}, u32[]{:S(2)}) copy-start(bf16[32,16,1024]{2,1,0:T(8,128)(2,1)S(1)} %fusion.3) | copy-start | bytes 3145732
  79.7 181.8 %all-reduce.9.cloned.1.call-start = ((), (), s32[]{:S(2)}) async-start(), calls=%async_computation.3 | async-start | bytes 524288 | tf_op jit(solution)/shard_map/psum | solution.py:87
  262.3 29.5 %copy-start.1 = (f32[256,256]{0,1:T(8,128)S(1)}, f32[256,256]{0,1:T(8,128)}, u32[]{:S(2)}) copy-start(f32[256,256]{0,1:T(8,128)} %all-reduce.9.cloned.1.call-done) | copy-start | bytes 786436
Sparse Core Ops, SparseCore 0:
  79.8 106.4 all-reduce.6
  188.8 72.6 all-reduce.8
